TPU v7x, 512 devices: a whole 4x8x8 slice. The times are simulated.
512 devices in a mesh: expert: 8 (over z_lo, x), fsdp: 64 (over z_hi, y, core).
Axes of the slice: x: 4, y: 8, z: 8 (z_hi: 4, z_lo: 2; z = z_hi * 2 + z_lo), core: 2. Of those that a mesh axis runs over, the one named last changes fastest.
Arguments:
- dense_rows: bfloat16 [128, 14336], P('fsdp', 'expert'), may hold values from -6 to 6
- noise: bfloat16 [8, 128, 14336], P('expert', 'fsdp'), may hold values from -6 to 6
- features: bfloat16 [8, 8192, 128], P('expert', 'fsdp'), may hold values from -16 to 16
- out_grads: bfloat16 [8, 8192, 14336], P('expert', 'fsdp'), may hold values from -1 to 1
Outputs:
- master: float32 [8, 128, 14336], P('expert', 'fsdp')
- first_moment: float32 [8, 128, 14336], P('expert', 'fsdp')
- second_moment: float32 [8, 128, 14336], P('expert', 'fsdp')
- expert_copy: bfloat16 [8, 128, 14336], P('expert')
All inputs are finite; a program needn't handle non-finite values.
Results may differ from a plain program's by a relative error of at most 0.004.
Values may be sent and summed in bfloat16 or wider, within the bound.
No kernel may reach another device: no remote copies, remote signals or barrier semaphores. Data moves between devices by JAX's collectives and lax.ppermute only.
A program may use at most 64 MiB of HBM per device.

v0:
```python
import jax
import jax.numpy as jnp
from jax import lax
from jax.sharding import PartitionSpec as P

noise_scale = 0.1
first_decay = 0.9
second_decay = 0.95
learn_rate = 0.2
weight_decay = 0.5
epsilon_adam = 1.0


def adamw(initial, gradient):
    first_moment = (1.0 - first_decay) * gradient
    second_moment = (1.0 - second_decay) * gradient * gradient
    update = (
        first_moment
        / (1.0 - first_decay)
        / (jnp.sqrt(second_moment / (1.0 - second_decay)) + epsilon_adam)
    )
    master = initial - learn_rate * (update + weight_decay * initial)
    return (master, first_moment, second_moment)


def body(dense_rows, noise, features, out_grads):
    dense_full = lax.all_gather(dense_rows, "expert", axis=1, tiled=True)
    initial = dense_full.astype(jnp.float32)[None] + noise_scale * noise.astype(jnp.float32)
    inputs_local = features[0]
    grads_local = out_grads[0]
    product = lax.dot_general(
        inputs_local, grads_local, (((0,), (0,)), ((), ())), preferred_element_type=jnp.float32
    )
    gradient = lax.psum_scatter(
        lax.optimization_barrier(product.astype(jnp.bfloat16)).astype(jnp.float32),
        "fsdp",
        scatter_dimension=0,
        tiled=True,
    )
    master, first_moment, second_moment = adamw(initial, gradient[None])
    expert_copy = lax.all_gather(master.astype(jnp.bfloat16), "fsdp", axis=1, tiled=True)
    return (master, first_moment, second_moment, expert_copy)


def solution(mesh):
    return jax.shard_map(
        body,
        mesh=mesh,
        in_specs=(
            P("fsdp", "expert"),
            P("expert", "fsdp", None),
            P("expert", "fsdp", None),
            P("expert", "fsdp", None),
        ),
        out_specs=(
            P("expert", "fsdp", None),
            P("expert", "fsdp", None),
            P("expert", "fsdp", None),
            P("expert", None, None),
        ),
        check_vma=False,
    )
```

profile of v0, /device:TPU:1, one launch (start us, length us, event | category | flops | bytes accessed | tf_op | source)
XLA Modules:
  0.0 503.9 jit_solution(10311162020342887844)
XLA Ops:
  7.2 0.0 copy-start
  7.2 0.0 all-gather.2.cloned.1.call-start
  7.2 0.7 copy-done
  7.9 5.0 convolution_convert_fusion
  12.9 0.0 copy-start.2
  12.9 0.0 copy-start.1
  13.0 339.0 %all-reduce.2 = f32[128,14336]{1,0:T(8,128)} all-reduce(bf16[128,14336]{1,0:T(8,128)(2,1)} %convolution_convert_fusion), channel_id=2, replica_groups=mesh['expert'=8,'fsdp'=64] {'fsdp'}, use_global_device_ids=true, to_apply=%region_0.0.clone | all-reduce | flops 1835008 | bytes 11010048
  352.0 0.0 copy-done.2
  352.0 29.0 %all_gather.6 = bf16[2,14336]{1,0:T(2,128)(2,1)S(1)} all-gather(bf16[2,1792]{1,0:T(2,128)(2,1)S(1)} %copy-done.2), channel_id=1, replica_groups=mesh['expert'=8,'fsdp'=64] {'expert'}, dimensions={1}, use_global_device_ids=true | all-gather | bytes 64512 | tf_op jit(solution)/shard_map/all_gather | solution.py:27
  381.0 1.3 dynamic-slice
  382.9 0.0 copy-done.1
  382.9 2.0 fusion.5
  384.9 0.7 copy.8
  385.7 0.0 all-gather.2.cloned.1.call-update
  385.7 1.8 fusion.3
  387.5 102.6 %all-gather.2.cloned.1.call-done = bf16[1,128,14336]{2,0,1:T(2,128)(2,1)} async-done(((bf16[1,2,14336]{2,0,1:T(2,128)(2,1)}), bf16[1,128,14336]{2,0,1:T(2,128)(2,1)}) %all-gather.2.cloned.1.call-update) | async-done | bytes 3670032 | tf_op jit(solution)/shard_map/all_gather | solution.py:41
  490.1 7.0 %copy.9 = bf16[1,128,14336]{2,1,0:T(8,128)(2,1)} copy(bf16[1,128,14336]{2,0,1:T(2,128)(2,1)} %all-gather.2.cloned.1.call-done) | data formatting | bytes 7340032
Async XLA Ops:
  7.2 0.8 copy-start
  7.2 482.9 %all-gather.2.cloned.1.call-start = ((), (), s32[]{:S(2)}) async-start(), calls=%async_computation | async-start | bytes 7454720 | tf_op jit(solution)/shard_map/all_gather | solution.py:41
  12.9 339.0 %copy-start.2 = (bf16[2,1792]{1,0:T(2,128)(2,1)S(1)}, bf16[2,1792]{1,0:T(2,128)(2,1)}, u32[]{:S(2)}) copy-start(bf16[2,1792]{1,0:T(2,128)(2,1)} %param.4) | copy-start | bytes 21508
  12.9 369.9 %copy-start.1 = (bf16[1,2,14336]{2,1,0:T(2,128)(2,1)S(1)}, bf16[1,2,14336]{2,1,0:T(2,128)(2,1)}, u32[]{:S(2)}) copy-start(bf16[1,2,14336]{2,1,0:T(2,128)(2,1)} %param.5) | copy-start | bytes 172036
Sparse Core Ops, SparseCore 0:
  385.8 104.2 all-gather.1
where the time goes:
time: 504 us
  blocking collectives  368 us (73%)
  waiting for transfers between devices  103 us (20%)
  between operations  14.7 us (3%)
  local copies, waits for them, and re-layouts  9.7 us (2%)
    unnamed x1, blocking collectives  339 us
    all_gather x1, waiting for transfers between devices, body(): lax.all_gather(master.astype(jnp.bfloat16), 'fsdp', axis=1, tiled=True)  103 us
    all_gather x1, blocking collectives, body(): dense_full = lax.all_gather(dense_rows, 'expert', axis=1, tiled=True)  29 us
  transfers between devices with their start and end apart: 1, of which 1 were waited for; matrix products, arithmetic and copies ran while one was open for 0% of the time, Pallas kernels for 0%

commit v1 on v0

--- a/solution.py
+++ b/solution.py
@@ -24,7 +24,10 @@
 
 
 def body(dense_rows, noise, features, out_grads):
-    dense_full = lax.all_gather(dense_rows, "expert", axis=1, tiled=True)
+    fix_rates = lambda xin: jnp.concatenate(
+        lax.all_to_all(jnp.stack([xin] * lax.axis_size("expert")), "expert", 0, 0), axis=1
+    )
+    dense_full = fix_rates(dense_rows)
     initial = dense_full.astype(jnp.float32)[None] + noise_scale * noise.astype(jnp.float32)
     inputs_local = features[0]
     grads_local = out_grads[0]

time: 504 us -> 482 us (0.956)
  blocking collectives: 368 us -> 338 us
  starting transfers between devices: 0.04 us -> 6.69 us
    all_gather x1 -> x0, blocking collectives: 29 us -> none  [body(): dense_full = lax.all_gather(dense_rows, 'expert', axis=1, tiled=True)]
    all_to_all x0 -> x1, starting transfers between devices: none -> 6.66 us  [body(): lax.all_to_all(jnp.stack([xin] * lax.axis_size('expert')), 'expert', 0, 0)]
  transfers between devices with their start and end apart: 1 -> 2, of which waited for: 1 -> 1; matrix products, arithmetic and copies ran while one was open for 0% -> 2% of each run, Pallas kernels for 0% -> 0%
where the time goes in v1:
time: 482 us; the launch traced here: 481 us
  blocking collectives  338 us (70%)
  waiting for transfers between devices  102 us (21%)
  between operations  14.7 us (3%)
  local copies, waits for them, and re-layouts  10.4 us (2%)
  starting transfers between devices  6.69 us (1%)
  matrix products  5.02 us (1%)
    unnamed x1, blocking collectives  338 us
    all_gather x1, waiting for transfers between devices, body(): lax.all_gather(master.astype(jnp.bfloat16), 'fsdp', axis=1, tiled=True)  102 us
  transfers between devices with their start and end apart: 2, of which 1 were waited for; matrix products, arithmetic and copies ran while one was open for 2% of the time, Pallas kernels for 0%

profile of v1, /device:TPU:1, one launch (start us, length us, event | category | flops | bytes accessed | tf_op | source)
XLA Modules:
  0.0 481.1 jit_solution(3516269588445589250)
XLA Ops:
  7.2 0.0 copy-start
  7.2 1.4 stack.2
  8.5 6.7 %all-to-all-start = ((bf16[8,2,1792]{2,1,0:T(2,128)(2,1)}), bf16[8,2,1792]{2,1,0:T(2,128)(2,1)S(1)}, u32[]{:S(2)}, u32[]{:S(2)}) async-start(bf16[8,2,1792]{2,1,0:T(2,128)(2,1)} %stack.2), calls=%async_computation | async-start | bytes 114688 | tf_op jit(solution)/shard_map/all_to_all | solution.py:28
  15.2 0.0 all-gather.2.cloned.1.call-start
  15.2 0.0 copy-done
  15.2 5.0 %convolution_convert_fusion = bf16[128,14336]{1,0:T(8,128)(2,1)} fusion(bf16[1,128,14336]{2,1,0:T(8,128)(2,1)} %param.7, bf16[1,128,128]{2,1,0:T(8,128)(2,1)S(1)} %copy-done), kind=kOutput, calls=%fused_computation | convolution fusion | flops 471597056 | bytes 7372800 | tf_op jit(solution)/shard_map/dot_general | solution.py:34
  20.3 0.0 copy-start.1
  20.3 337.9 %all-reduce.2 = f32[128,14336]{1,0:T(8,128)} all-reduce(bf16[128,14336]{1,0:T(8,128)(2,1)} %convolution_convert_fusion), channel_id=2, replica_groups=mesh['expert'=8,'fsdp'=64] {'fsdp'}, use_global_device_ids=true, to_apply=%region_0.0.clone | all-reduce | flops 1835008 | bytes 11010048
  358.2 1.3 dynamic-slice
  360.1 0.0 all-to-all-done
  360.2 0.0 copy-done.1
  360.2 2.0 fusion.5
  362.2 0.7 copy.8
  363.0 0.0 all-gather.2.cloned.1.call-update
  363.0 1.8 fusion.3
  364.8 102.4 %all-gather.2.cloned.1.call-done = bf16[1,128,14336]{2,0,1:T(2,128)(2,1)} async-done(((bf16[1,2,14336]{2,0,1:T(2,128)(2,1)}), bf16[1,128,14336]{2,0,1:T(2,128)(2,1)}) %all-gather.2.cloned.1.call-update) | async-done | bytes 3670032 | tf_op jit(solution)/shard_map/all_gather | solution.py:44
  467.2 7.0 %copy.9 = bf16[1,128,14336]{2,1,0:T(8,128)(2,1)} copy(bf16[1,128,14336]{2,0,1:T(2,128)(2,1)} %all-gather.2.cloned.1.call-done) | data formatting | bytes 7340032
  (1 shorter events, 0.0 us)
Async XLA Ops:
  7.2 8.1 %copy-start = (bf16[1,128,128]{2,1,0:T(8,128)(2,1)S(1)}, bf16[1,128,128]{2,1,0:T(8,128)(2,1)}, u32[]{:S(2)}) copy-start(bf16[1,128,128]{2,1,0:T(8,128)(2,1)} %param.6) | copy-start | bytes 98308
  8.5 351.6 %all-to-all-start = ((bf16[8,2,1792]{2,1,0:T(2,128)(2,1)}), bf16[8,2,1792]{2,1,0:T(2,128)(2,1)S(1)}, u32[]{:S(2)}, u32[]{:S(2)}) async-start(bf16[8,2,1792]{2,1,0:T(2,128)(2,1)} %stack.2), calls=%async_computation | async-start | bytes 114688 | tf_op jit(solution)/shard_map/all_to_all | solution.py:28
  15.2 452.0 %all-gather.2.cloned.1.call-start = ((), (), s32[]{:S(2)}) async-start(), calls=%async_computation.1 | async-start | bytes 7454720 | tf_op jit(solution)/shard_map/all_gather | solution.py:44
  20.3 339.9 %copy-start.1 = (bf16[1,2,14336]{2,1,0:T(2,128)(2,1)S(1)}, bf16[1,2,14336]{2,1,0:T(2,128)(2,1)}, u32[]{:S(2)}) copy-start(bf16[1,2,14336]{2,1,0:T(2,128)(2,1)} %param.5) | copy-start | bytes 172036
Sparse Core Ops, SparseCore 0:
  363.1 104.0 all-gather.1
